TPU v7x, 32 devices: a whole 2x2x4 slice. The times are simulated.
32 devices in a mesh: dp: 8 (over z, y), mp: 4 (over x, core).
Axes of the slice: x: 2, y: 2, z: 4, core: 2. Of those that a mesh axis runs over, the one named last changes fastest.
Arguments:
- hidden: bfloat16 [16, 64, 3584], P('dp', None, 'mp'), may hold values from -6 to 6
- rewards: float32 [16, 64], P('dp'), may hold values from -6 to 6
- actions: int32 [16, 64], P('dp'), may hold values from 0 to 152063, as said below
- lengths: int32 [16], P('dp'), may hold values from 1 to 64, 512 in all
- table: bfloat16 [152064, 3584], P('dp', 'mp'), may hold values from -0.09375 to 0.09375
- q_one: bfloat16 [3584, 3584], P('dp', 'mp'), may hold values from -0.09375 to 0.09375
- q_two: bfloat16 [3584, 3584], P('dp', 'mp'), may hold values from -0.09375 to 0.09375
- t_one: bfloat16 [3584, 3584], P('dp', 'mp'), may hold values from -0.09375 to 0.09375
- t_two: bfloat16 [3584, 3584], P('dp', 'mp'), may hold values from -0.09375 to 0.09375
- value_weight: bfloat16 [3584], P('mp'), may hold values from -0.09375 to 0.09375
- value_bias: float32 [1], replicated, may hold values from -3 to 3
Outputs:
- loss: float32 [], replicated
- grad_q_one: float32 [3584, 3584], P('dp', 'mp')
- grad_q_two: float32 [3584, 3584], P('dp', 'mp')
- grad_value: float32 [3584], P('mp')
- grad_bias: float32 [1], replicated
- target_one: bfloat16 [3584, 3584], P('dp', 'mp')
- target_two: bfloat16 [3584, 3584], P('dp', 'mp')
Inputs may be any that keep to these rules, and one draw needn't show every extreme that they name: `actions`: among the 128 positions of the prompts of one index of dp, exactly 16 action ids fall in each of the aligned blocks of 19008 vocabulary rows.
All inputs are finite; a program needn't handle non-finite values. No bound on the sum of `lengths` on one device may be relied on, other than what follows from the above.
Results may differ from a plain program's by a relative error of at most 0.0045.
Values may be sent and summed in bfloat16 or wider, within the bound.
A program may use at most 192 MiB of HBM per device.

v0:
```python
import jax
import jax.numpy as jnp
from jax import lax
from jax.sharding import PartitionSpec as P

discount = 0.99
expectile = 0.7
polyak_rate = 0.005
f32 = jnp.float32
bf16 = jnp.bfloat16


def head_gelu(inputs):
    return jax.nn.gelu(inputs, approximate=True)


def slope(preact, upstream):
    _, pullback = jax.vjp(head_gelu, preact)
    return pullback(upstream)[0]


def pick(mask, row):
    return jnp.sum(jnp.where(mask, row[None, :], jnp.zeros((), row.dtype)), axis=1)


def on_device(
    hidden, rewards, actions, lengths, table, q_one, q_two, t_one, t_two, value_weight, value_bias
):
    dp = lax.axis_size("dp")
    me = lax.axis_index("dp")
    prompts, slots, width = hidden.shape
    own = prompts * slots
    total = own * dp
    packed = total // 2
    share = packed // dp
    cols = q_one.shape[1]
    rows = q_one.shape[0]
    local_rows = table.shape[0]
    local_flat = hidden.reshape(own, width)
    stacked = jnp.concatenate([local_flat, value_weight.reshape(1, width)], axis=0)
    wide = lax.all_gather(stacked, "mp", axis=1, tiled=True)
    flat, value_row = (wide[:own], wide[own:])
    values = (
        jnp.sum(flat.astype(f32) * value_row.astype(f32), axis=1).reshape(prompts, slots)
        + value_bias[0]
    )
    positions = jnp.arange(slots, dtype=jnp.int32)[None, :]
    follows = positions + 1 < lengths[:, None]
    shifted = jnp.concatenate([values[:, 1:], jnp.zeros_like(values[:, :1])], axis=1)
    target = rewards + discount * jnp.where(follows, shifted, 0.0)
    ints = jnp.concatenate([actions, lengths[:, None]], axis=1)
    all_ints = lax.all_gather(ints, "dp", axis=0, tiled=True)
    all_lengths = all_ints[:, slots]
    ids = all_ints[:, :slots].reshape(total)
    facts = jnp.stack([target.reshape(own), values.reshape(own)])
    all_facts = lax.all_gather(facts, "dp", axis=1, tiled=True)
    count = jnp.sum(all_lengths).astype(f32)
    factor = 1.0 / count
    prompt_ids = jnp.arange(prompts * dp, dtype=jnp.int32)
    offsets = jnp.sum(
        jnp.where(prompt_ids[None, :] < prompt_ids[:, None], all_lengths[None, :], 0), axis=1
    )
    place = jnp.where(positions < all_lengths[:, None], offsets[:, None] + positions, -1).reshape(
        total
    )
    own_slots = jnp.arange(share, dtype=jnp.int32)[:, None] + me * share
    own_mask = own_slots == place[None, :]
    holders = ids // local_rows
    by_source = holders.reshape(dp, own)
    order = jnp.arange(own, dtype=jnp.int32)
    earlier = (by_source[:, :, None] == by_source[:, None, :]) & (
        order[None, None, :] < order[None, :, None]
    )
    per_source = own // dp
    rank = (
        jnp.sum(earlier.astype(jnp.int32), axis=2)
        + jnp.arange(dp, dtype=jnp.int32)[:, None] * per_source
    ).reshape(total)
    where_held = holders * own + rank
    wanted = jnp.arange(own, dtype=jnp.int32)[:, None] + me * own == where_held[None, :]
    requests = pick(wanted, ids - me * local_rows)
    found = table[requests]
    all_found = lax.all_gather(found, "dp", axis=0, tiled=True)
    seat = pick(own_mask, where_held)
    seat_mask = (jnp.arange(total, dtype=jnp.int32)[None, :] == seat[:, None]).astype(bf16)
    embed = jnp.dot(seat_mask, all_found, preferred_element_type=f32)
    spread = lax.all_to_all(flat, "dp", split_axis=1, concat_axis=0, tiled=True)
    pack_mask = (jnp.arange(packed, dtype=jnp.int32)[:, None] == place[None, :]).astype(bf16)
    held = jnp.dot(pack_mask, spread, preferred_element_type=f32).astype(bf16)
    partial = jnp.concatenate(
        [
            jnp.dot(held, weight, preferred_element_type=f32).astype(bf16)
            for weight in (q_one, q_two, t_one, t_two)
        ],
        axis=1,
    )
    swapped = lax.all_to_all(partial, "dp", split_axis=0, concat_axis=0, tiled=True)
    pre = jnp.sum(swapped.reshape(dp, share, 4 * cols).astype(f32), axis=0)
    pres = [pre[:, k * cols : (k + 1) * cols] for k in range(4)]
    scores = jnp.stack([jnp.sum(head_gelu(p) * embed, axis=1) for p in pres])
    board = lax.dynamic_update_slice(
        jnp.zeros((4, packed), f32), scores, (jnp.zeros((), jnp.int32), me * share)
    )
    all_scores = lax.psum(board, ("dp", "mp"))
    pack_bool = jnp.arange(packed, dtype=jnp.int32)[:, None] == place[None, :]
    goal = pick(pack_bool, all_facts[0])
    worth = pick(pack_bool, all_facts[1])
    lowest = jnp.minimum(all_scores[2], all_scores[3])
    spread_to = lowest - worth
    weights = jnp.where(spread_to < 0.0, 1.0 - expectile, expectile)
    err_one = all_scores[0] - goal
    err_two = all_scores[1] - goal
    loss = jnp.sum(err_one * err_one + err_two * err_two + weights * spread_to * spread_to) * factor
    grad_values = -2.0 * weights * spread_to
    bias_grad = jnp.sum(grad_values) * factor
    up_one = lax.dynamic_slice(2.0 * err_one, (me * share,), (share,))
    up_two = lax.dynamic_slice(2.0 * err_two, (me * share,), (share,))
    back = jnp.concatenate(
        [
            slope(pres[0], up_one[:, None] * embed).astype(bf16),
            slope(pres[1], up_two[:, None] * embed).astype(bf16),
        ],
        axis=1,
    )
    all_back = lax.all_gather(back, "dp", axis=0, tiled=True)
    dims = (((0,), (0,)), ((), ()))
    head_one = lax.dot_general(held, all_back[:, :cols], dims, preferred_element_type=f32) * factor
    head_two = lax.dot_general(held, all_back[:, cols:], dims, preferred_element_type=f32) * factor
    own_place = lax.dynamic_slice(place, (me * own,), (own,))
    own_errors = pick(
        own_place[:, None] == jnp.arange(packed, dtype=jnp.int32)[None, :], grad_values
    )
    value_part = jnp.sum(own_errors[:, None] * local_flat.astype(f32), axis=0)
    value_grad = lax.psum(value_part * factor, "dp")
    new_one = ((1.0 - polyak_rate) * t_one.astype(f32) + polyak_rate * q_one.astype(f32)).astype(
        bf16
    )
    new_two = ((1.0 - polyak_rate) * t_two.astype(f32) + polyak_rate * q_two.astype(f32)).astype(
        bf16
    )
    return (loss, head_one, head_two, value_grad, bias_grad.reshape(1), new_one, new_two)


def solution(mesh):
    in_specs = (
        P("dp", None, "mp"),
        P("dp", None),
        P("dp", None),
        P("dp"),
        P("dp", "mp"),
        P("dp", "mp"),
        P("dp", "mp"),
        P("dp", "mp"),
        P("dp", "mp"),
        P("mp"),
        P(),
    )
    out_specs = (P(), P("dp", "mp"), P("dp", "mp"), P("mp"), P(), P("dp", "mp"), P("dp", "mp"))
    return jax.shard_map(
        on_device, mesh=mesh, in_specs=in_specs, out_specs=out_specs, check_vma=False
    )
```

profile of v0, /device:TPU:0, one launch (start us, length us, event | category | flops | bytes accessed | tf_op | source)
XLA Modules:
  0.0 288.4 jit_solution(14997182306145007077)
XLA Ops:
  7.9 1.0 pad_maximum_fusion.1
  8.8 11.1 %all_gather.16 = bf16[129,3584]{1,0:T(8,128)(2,1)S(1)} all-gather(bf16[129,896]{1,0:T(8,128)(2,1)S(1)} %pad_maximum_fusion.1), channel_id=1, replica_groups=mesh['dp'=8,'mp'=4] {'mp'}, dimensions={1}, use_global_device_ids=true | all-gather | bytes 1155840 | tf_op jit(solution)/shard_map/all_gather | solution.py:41
  20.0 1.3 copy.34
  21.3 5.8 %all-to-all-start = ((bf16[128,8,448]{0,2,1:T(8,128)(2,1)}), bf16[128,8,448]{0,2,1:T(8,128)(2,1)S(1)}, u32[]{:S(2)}, u32[]{:S(2)}) async-start(bf16[128,8,448]{0,2,1:T(8,128)(2,1)} %bitcast.5), calls=%async_computation | async-start | bytes 1835008 | tf_op jit(solution)/shard_map/all_to_all | solution.py:87
  27.3 30.6 %all-gather.1 = s32[8,2,65]{2,1,0:T(2,128)S(1)} all-gather(s32[1,2,65]{2,1,0:T(2,128)S(1)} %add_bitcast_fusion), channel_id=1, replica_groups=mesh['dp'=8,'mp'=4] {'dp'}, dimensions={0}, use_global_device_ids=true | all-gather | bytes 4680 | tf_op jit(solution)/shard_map/all_gather | solution.py:52
  58.9 0.7 fusion.1
  59.6 0.7 convolution_convert_fusion
  60.8 0.7 convolution_convert_fusion.1
  61.9 0.7 convolution_convert_fusion.2
  63.1 0.7 convolution_convert_fusion.3
  63.8 2.0 pad_maximum_fusion
  65.8 4.5 %all-to-all-start.1 = ((bf16[8,64,3584]{2,1,0:T(8,128)(2,1)}), bf16[8,64,3584]{2,1,0:T(8,128)(2,1)}, u32[]{:S(2)}, u32[]{:S(2)}) async-start(bf16[8,64,3584]{2,1,0:T(8,128)(2,1)} %bitcast.50), calls=%async_computation.1 | async-start | bytes 7340032 | tf_op jit(solution)/shard_map/all_to_all | solution.py:97
  71.5 2.9 %gather_fusion = bf16[128,896]{1,0:T(8,128)(2,1)} fusion(bf16[19008,896]{1,0:T(8,128)(2,1)} %param.15, s32[1024]{0:T(1024)S(1)} %pad_clamp_fusion), kind=kCustom, calls=%fused_computation | custom fusion | bytes 459264 | tf_op jit(solution)/shard_map/gather | solution.py:82
  75.8 83.3 %all_gather.18 = f32[2,1024]{1,0:T(2,128)S(1)} all-gather(f32[2,128]{1,0:T(2,128)S(1)} %pad_maximum_fusion.4), channel_id=1, replica_groups=mesh['dp'=8,'mp'=4] {'dp'}, dimensions={1}, use_global_device_ids=true | all-gather | bytes 9216 | tf_op jit(solution)/shard_map/all_gather | solution.py:56
  160.0 12.1 %all-to-all-done.1 = bf16[8,64,3584]{2,1,0:T(8,128)(2,1)} async-done(((bf16[8,64,3584]{2,1,0:T(8,128)(2,1)}), bf16[8,64,3584]{2,1,0:T(8,128)(2,1)}, u32[]{:S(2)}, u32[]{:S(2)}) %all-to-all-start.1) | async-done | bytes 3670048 | tf_op jit(solution)/shard_map/all_to_all | solution.py:97
  172.1 2.6 convert_reduce_fusion
  174.7 2.3 multiply_reduce_fusion.3
  177.2 48.2 %psum.14 = f32[4,512]{1,0:T(4,128)S(1)} all-reduce(f32[4,512]{1,0:T(4,128)S(1)} %dynamic_update_slice.3), channel_id=1, replica_groups=mesh['dp'=8,'mp'=4] {'dp','mp'}, use_global_device_ids=true, to_apply=%region_9.10 | all-reduce | flops 2048 | bytes 16384 | tf_op jit(solution)/shard_map/psum | solution.py:104
  226.6 0.7 pad_maximum_fusion.2
  228.1 3.2 %add_convert_fusion = (bf16[448,896]{1,0:T(8,128)(2,1)}, bf16[448,896]{1,0:T(8,128)(2,1)}) fusion(bf16[448,896]{1,0:T(8,128)(2,1)} %param.17, bf16[448,896]{1,0:T(8,128)(2,1)S(1)} %copy-done.2, bf16[448,896]{1,0:T(8,128)(2,1)} %param.16, bf16[448,896]{1,0:T(8,128)(2,1)S(1)} %copy-done.3), kind=kLoop, calls=%fused_computation.8 | loop fusion | flops 4816896 | bytes 4816896 | tf_op jit(solution)/shard_map/convert_element_type | solution.py:138
  233.0 21.8 %psum.15 = f32[896]{0:T(1024)} all-reduce(f32[896]{0:T(1024)S(1)} %broadcast_multiply_fusion), channel_id=1, replica_groups=mesh['dp'=8,'mp'=4] {'dp'}, use_global_device_ids=true, to_apply=%region_17.18 | all-reduce | flops 896 | bytes 7168 | tf_op jit(solution)/shard_map/psum | solution.py:134
  254.8 19.6 %all-gather.5.cloned.1.call-done = bf16[512,1792]{1,0:T(8,128)(2,1)} async-done(((bf16[64,1792]{1,0:T(8,128)(2,1)}), bf16[512,1792]{1,0:T(8,128)(2,1)}) %all-gather.5.cloned.1.call-update) | async-done | bytes 1835024 | tf_op jit(solution)/shard_map/all_gather | solution.py:125
  274.4 3.1 %convolution_multiply_fusion.1 = f32[448,896]{1,0:T(8,128)} fusion(bf16[512,448]{0,1:T(8,128)(2,1)S(1)} %fusion.1, bf16[512,1792]{1,0:T(8,128)(2,1)} %all-gather.5.cloned.1.call-done, f32[]{:T(128)S(6)} %div.30), kind=kOutput, calls=%fused_computation.11 | convolution fusion | flops 411443200 | bytes 2981892 | tf_op jit(solution)/shard_map/dot_general | solution.py:127
  277.5 1.8 convolution_multiply_fusion
  (76 shorter events, 7.7 us)
Async XLA Ops:
  20.0 7.1 %copy-start.8 = (s32[2]{0:T(128)S(1)}, s32[2]{0:T(128)}, u32[]{:S(2)}) copy-start(s32[2]{0:T(128)} %param.14) | copy-start | bytes 28
  20.0 7.2 %copy-start.6 = (s32[2,64]{1,0:T(2,128)S(1)}, s32[2,64]{1,0:T(2,128)}, u32[]{:S(2)}) copy-start(s32[2,64]{1,0:T(2,128)} %param.13) | copy-start | bytes 1540
  21.3 37.6 %all-to-all-start = ((bf16[128,8,448]{0,2,1:T(8,128)(2,1)}), bf16[128,8,448]{0,2,1:T(8,128)(2,1)S(1)}, u32[]{:S(2)}, u32[]{:S(2)}) async-start(bf16[128,8,448]{0,2,1:T(8,128)(2,1)} %bitcast.5), calls=%async_computation | async-start | bytes 1835008 | tf_op jit(solution)/shard_map/all_to_all | solution.py:87
  27.1 32.5 %copy-start.2 = (bf16[448,896]{1,0:T(8,128)(2,1)S(1)}, bf16[448,896]{1,0:T(8,128)(2,1)}, u32[]{:S(2)}) copy-start(bf16[448,896]{1,0:T(8,128)(2,1)} %param.19) | copy-start | bytes 2408452
  59.6 1.1 copy-start.3
  60.8 1.1 copy-start.4
  61.9 1.1 copy-start.5
  65.8 106.3 %all-to-all-start.1 = ((bf16[8,64,3584]{2,1,0:T(8,128)(2,1)}), bf16[8,64,3584]{2,1,0:T(8,128)(2,1)}, u32[]{:S(2)}, u32[]{:S(2)}) async-start(bf16[8,64,3584]{2,1,0:T(8,128)(2,1)} %bitcast.50), calls=%async_computation.1 | async-start | bytes 7340032 | tf_op jit(solution)/shard_map/all_to_all | solution.py:97
  70.3 5.3 %copy-start.7 = (f32[2,64]{1,0:T(2,128)S(1)}, f32[2,64]{1,0:T(2,128)}, u32[]{:S(2)}) copy-start(f32[2,64]{1,0:T(2,128)} %param.12) | copy-start | bytes 1540
  70.3 104.4 %all-gather.7.cloned.1.call-start = ((), (), s32[]{:S(2)}) async-start(), calls=%async_computation.3 | async-start | bytes 2064384 | tf_op jit(solution)/shard_map/all_gather | solution.py:83
  74.4 199.9 %all-gather.5.cloned.1.call-start = ((), (), s32[]{:S(2)}) async-start(), calls=%async_computation.2 | async-start | bytes 2064384 | tf_op jit(solution)/shard_map/all_gather | solution.py:125
  228.1 4.8 %copy-start.1 = (bf16[2,64,896]{2,1,0:T(8,128)(2,1)S(1)}, bf16[2,64,896]{2,1,0:T(8,128)(2,1)}, u32[]{:S(2)}) copy-start(bf16[2,64,896]{2,1,0:T(8,128)(2,1)} %param.11) | copy-start | bytes 688132
  274.4 3.1 %copy-start = (bf16[512,1792]{1,0:T(8,128)(2,1)S(1)}, bf16[512,1792]{1,0:T(8,128)(2,1)}, u32[]{:S(2)}) copy-start(bf16[512,1792]{1,0:T(8,128)(2,1)} %all-gather.5.cloned.1.call-done) | copy-start | bytes 5505028
Sparse Core Ops, SparseCore 0:
  74.5 86.5 all-gather.6
  227.4 46.9 all-gather.4
where the time goes:
time: 289 us; the launch traced here: 288 us
  blocking collectives  195 us (67%)
  waiting for transfers between devices  31.8 us (11%)
  between operations  19.2 us (7%)
  other arithmetic  13.7 us (5%)
  matrix products  10.8 us (4%)
  starting transfers between devices  10.4 us (4%)
  local copies, waits for them, and re-layouts  7.53 us (3%)
    all_gather x1, blocking collectives, on_device(): all_facts = lax.all_gather(facts, 'dp', axis=1, tiled=True)  83.3 us
    psum x1, blocking collectives, on_device(): all_scores = lax.psum(board, ('dp', 'mp'))  48.2 us
    all_gather x1, blocking collectives, on_device(): all_ints = lax.all_gather(ints, 'dp', axis=0, tiled=True)  30.6 us
    psum x1, blocking collectives, on_device(): value_grad = lax.psum(value_part * factor, 'dp')  21.8 us
    all_gather x1, waiting for transfers between devices, on_device(): all_back = lax.all_gather(back, 'dp', axis=0, tiled=True)  19.6 us
    all_to_all x1, waiting for transfers between devices, on_device(): lax.all_to_all(partial, 'dp', split_axis=0, concat_axis=0, tiled=True)  12.1 us
    all_gather x1, blocking collectives, on_device(): wide = lax.all_gather(stacked, 'mp', axis=1, tiled=True)  11.1 us
    all_to_all x1, starting transfers between devices, on_device(): spread = lax.all_to_all(flat, 'dp', split_axis=1, concat_axis=0, tiled=True)  5.83 us
  transfers between devices with their start and end apart: 4, of which 2 were waited for; matrix products, arithmetic and copies ran while one was open for 5% of the time, Pallas kernels for 0%

commit v1 on v0

--- a/solution.py
+++ b/solution.py
@@ -101,7 +101,8 @@
     board = lax.dynamic_update_slice(
         jnp.zeros((4, packed), f32), scores, (jnp.zeros((), jnp.int32), me * share)
     )
-    all_scores = lax.psum(board, ("dp", "mp"))
+    parts = lax.all_gather(board, ("dp", "mp"))
+    all_scores = jnp.sum(parts, axis=0)
     pack_bool = jnp.arange(packed, dtype=jnp.int32)[:, None] == place[None, :]
     goal = pick(pack_bool, all_facts[0])
     worth = pick(pack_bool, all_facts[1])

time: 289 us -> 286 us (0.990)
  blocking collectives: 195 us -> 192 us
    all_gather x0 -> x1, blocking collectives: none -> 48.9 us  [on_device(): parts = lax.all_gather(board, ('dp', 'mp'))]
    psum x1 -> x0, blocking collectives: 48.2 us -> none  [on_device(): all_scores = lax.psum(board, ('dp', 'mp'))]
    psum x1, blocking collectives: 21.8 us -> 17.8 us  [on_device(): value_grad = lax.psum(value_part * factor, 'dp')]
where the time goes in v1:
time: 286 us; the launch traced here: 285 us
  blocking collectives  192 us (67%)
  waiting for transfers between devices  31.6 us (11%)
  between operations  19.2 us (7%)
  other arithmetic  13.8 us (5%)
  matrix products  10.8 us (4%)
  starting transfers between devices  10.4 us (4%)
  local copies, waits for them, and re-layouts  7.53 us (3%)
    all_gather x1, blocking collectives, on_device(): all_facts = lax.all_gather(facts, 'dp', axis=1, tiled=True)  83.3 us
    all_gather x1, blocking collectives, on_device(): parts = lax.all_gather(board, ('dp', 'mp'))  48.9 us
    all_gather x1, blocking collectives, on_device(): all_ints = lax.all_gather(ints, 'dp', axis=0, tiled=True)  30.6 us
    all_gather x1, waiting for transfers between devices, on_device(): all_back = lax.all_gather(back, 'dp', axis=0, tiled=True)  19.4 us
    psum x1, blocking collectives, on_device(): value_grad = lax.psum(value_part * factor, 'dp')  17.8 us
    all_to_all x1, waiting for transfers between devices, on_device(): lax.all_to_all(partial, 'dp', split_axis=0, concat_axis=0, tiled=True)  12.1 us
    all_gather x1, blocking collectives, on_device(): wide = lax.all_gather(stacked, 'mp', axis=1, tiled=True)  11.1 us
    all_to_all x1, starting transfers between devices, on_device(): spread = lax.all_to_all(flat, 'dp', split_axis=1, concat_axis=0, tiled=True)  5.83 us
  transfers between devices with their start and end apart: 4, of which 2 were waited for; matrix products, arithmetic and copies ran while one was open for 5% of the time, Pallas kernels for 0%

profile of v1, /device:TPU:0, one launch (start us, length us, event | category | flops | bytes accessed | tf_op | source)
XLA Modules:
  0.0 284.9 jit_solution(13683743620185590132)
XLA Ops:
  7.9 1.0 pad_maximum_fusion.1
  8.8 11.1 %all_gather.22 = bf16[129,3584]{1,0:T(8,128)(2,1)S(1)} all-gather(bf16[129,896]{1,0:T(8,128)(2,1)S(1)} %pad_maximum_fusion.1), channel_id=1, replica_groups=mesh['dp'=8,'mp'=4] {'mp'}, dimensions={1}, use_global_device_ids=true | all-gather | bytes 1155840 | tf_op jit(solution)/shard_map/all_gather | solution.py:41
  20.0 1.3 copy.34
  21.3 5.8 %all-to-all-start = ((bf16[128,8,448]{0,2,1:T(8,128)(2,1)}), bf16[128,8,448]{0,2,1:T(8,128)(2,1)S(1)}, u32[]{:S(2)}, u32[]{:S(2)}) async-start(bf16[128,8,448]{0,2,1:T(8,128)(2,1)} %bitcast.5), calls=%async_computation | async-start | bytes 1835008 | tf_op jit(solution)/shard_map/all_to_all | solution.py:87
  27.3 30.6 %all-gather.1 = s32[8,2,65]{2,1,0:T(2,128)S(1)} all-gather(s32[1,2,65]{2,1,0:T(2,128)S(1)} %add_bitcast_fusion), channel_id=1, replica_groups=mesh['dp'=8,'mp'=4] {'dp'}, dimensions={0}, use_global_device_ids=true | all-gather | bytes 4680 | tf_op jit(solution)/shard_map/all_gather | solution.py:52
  58.9 0.7 fusion.1
  59.6 0.7 convolution_convert_fusion
  60.8 0.7 convolution_convert_fusion.1
  61.9 0.7 convolution_convert_fusion.2
  63.1 0.7 convolution_convert_fusion.3
  63.8 2.0 pad_maximum_fusion
  65.8 4.5 %all-to-all-start.1 = ((bf16[8,64,3584]{2,1,0:T(8,128)(2,1)}), bf16[8,64,3584]{2,1,0:T(8,128)(2,1)}, u32[]{:S(2)}, u32[]{:S(2)}) async-start(bf16[8,64,3584]{2,1,0:T(8,128)(2,1)} %bitcast.52), calls=%async_computation.1 | async-start | bytes 7340032 | tf_op jit(solution)/shard_map/all_to_all | solution.py:97
  71.5 2.9 %gather_fusion = bf16[128,896]{1,0:T(8,128)(2,1)} fusion(bf16[19008,896]{1,0:T(8,128)(2,1)} %param.15, s32[1024]{0:T(1024)S(1)} %pad_clamp_fusion), kind=kCustom, calls=%fused_computation | custom fusion | bytes 459264 | tf_op jit(solution)/shard_map/gather | solution.py:82
  75.8 83.3 %all_gather.26 = f32[2,1024]{1,0:T(2,128)S(1)} all-gather(f32[2,128]{1,0:T(2,128)S(1)} %pad_maximum_fusion.3), channel_id=1, replica_groups=mesh['dp'=8,'mp'=4] {'dp'}, dimensions={1}, use_global_device_ids=true | all-gather | bytes 9216 | tf_op jit(solution)/shard_map/all_gather | solution.py:56
  160.0 12.1 %all-to-all-done.1 = bf16[8,64,3584]{2,1,0:T(8,128)(2,1)} async-done(((bf16[8,64,3584]{2,1,0:T(8,128)(2,1)}), bf16[8,64,3584]{2,1,0:T(8,128)(2,1)}, u32[]{:S(2)}, u32[]{:S(2)}) %all-to-all-start.1) | async-done | bytes 3670048 | tf_op jit(solution)/shard_map/all_to_all | solution.py:97
  172.1 2.6 convert_reduce_fusion
  174.7 2.3 multiply_reduce_fusion.3
  177.2 48.9 %all_gather.25 = f32[32,4,512]{2,1,0:T(4,128)S(1)} all-gather(f32[1,4,512]{2,1,0:T(4,128)S(1)} %dynamic_update_slice.4), channel_id=1, replica_groups=mesh['dp'=8,'mp'=4] {'dp','mp'}, dimensions={0}, use_global_device_ids=true | all-gather | bytes 270336 | tf_op jit(solution)/shard_map/all_gather | solution.py:104
  227.3 0.7 pad_maximum_fusion.2
  228.8 3.2 %add_convert_fusion = (bf16[448,896]{1,0:T(8,128)(2,1)}, bf16[448,896]{1,0:T(8,128)(2,1)}) fusion(bf16[448,896]{1,0:T(8,128)(2,1)} %param.17, bf16[448,896]{1,0:T(8,128)(2,1)S(1)} %copy-done.2, bf16[448,896]{1,0:T(8,128)(2,1)} %param.16, bf16[448,896]{1,0:T(8,128)(2,1)S(1)} %copy-done.3), kind=kLoop, calls=%fused_computation.8 | loop fusion | flops 4816896 | bytes 4816896 | tf_op jit(solution)/shard_map/convert_element_type | solution.py:139
  233.7 17.8 %psum.7 = f32[896]{0:T(1024)} all-reduce(f32[896]{0:T(1024)S(1)} %broadcast_multiply_fusion), channel_id=1, replica_groups=mesh['dp'=8,'mp'=4] {'dp'}, use_global_device_ids=true, to_apply=%region_17.18 | all-reduce | flops 896 | bytes 7168 | tf_op jit(solution)/shard_map/psum | solution.py:135
  251.5 19.4 %all-gather.5.cloned.1.call-done = bf16[512,1792]{1,0:T(8,128)(2,1)} async-done(((bf16[64,1792]{1,0:T(8,128)(2,1)}), bf16[512,1792]{1,0:T(8,128)(2,1)}) %all-gather.5.cloned.1.call-update) | async-done | bytes 1835024 | tf_op jit(solution)/shard_map/all_gather | solution.py:126
  270.9 3.1 %convolution_multiply_fusion.1 = f32[448,896]{1,0:T(8,128)} fusion(bf16[512,448]{0,1:T(8,128)(2,1)S(1)} %fusion.1, bf16[512,1792]{1,0:T(8,128)(2,1)} %all-gather.5.cloned.1.call-done, f32[]{:T(128)S(6)} %div.30), kind=kOutput, calls=%fused_computation.11 | convolution fusion | flops 411443200 | bytes 2981892 | tf_op jit(solution)/shard_map/dot_general | solution.py:128
  274.0 1.8 convolution_multiply_fusion
  (77 shorter events, 7.8 us)
Async XLA Ops:
  20.0 7.1 %copy-start.8 = (s32[2]{0:T(128)S(1)}, s32[2]{0:T(128)}, u32[]{:S(2)}) copy-start(s32[2]{0:T(128)} %param.14) | copy-start | bytes 28
  20.0 7.2 %copy-start.6 = (s32[2,64]{1,0:T(2,128)S(1)}, s32[2,64]{1,0:T(2,128)}, u32[]{:S(2)}) copy-start(s32[2,64]{1,0:T(2,128)} %param.13) | copy-start | bytes 1540
  21.3 37.6 %all-to-all-start = ((bf16[128,8,448]{0,2,1:T(8,128)(2,1)}), bf16[128,8,448]{0,2,1:T(8,128)(2,1)S(1)}, u32[]{:S(2)}, u32[]{:S(2)}) async-start(bf16[128,8,448]{0,2,1:T(8,128)(2,1)} %bitcast.5), calls=%async_computation | async-start | bytes 1835008 | tf_op jit(solution)/shard_map/all_to_all | solution.py:87
  27.1 32.5 %copy-start.2 = (bf16[448,896]{1,0:T(8,128)(2,1)S(1)}, bf16[448,896]{1,0:T(8,128)(2,1)}, u32[]{:S(2)}) copy-start(bf16[448,896]{1,0:T(8,128)(2,1)} %param.19) | copy-start | bytes 2408452
  59.6 1.1 copy-start.3
  60.8 1.1 copy-start.4
  61.9 1.1 copy-start.5
  65.8 106.3 %all-to-all-start.1 = ((bf16[8,64,3584]{2,1,0:T(8,128)(2,1)}), bf16[8,64,3584]{2,1,0:T(8,128)(2,1)}, u32[]{:S(2)}, u32[]{:S(2)}) async-start(bf16[8,64,3584]{2,1,0:T(8,128)(2,1)} %bitcast.52), calls=%async_computation.1 | async-start | bytes 7340032 | tf_op jit(solution)/shard_map/all_to_all | solution.py:97
  70.3 5.3 %copy-start.7 = (f32[2,64]{1,0:T(2,128)S(1)}, f32[2,64]{1,0:T(2,128)}, u32[]{:S(2)}) copy-start(f32[2,64]{1,0:T(2,128)} %param.12) | copy-start | bytes 1540
  70.3 104.4 %all-gather.7.cloned.1.call-start = ((), (), s32[]{:S(2)}) async-start(), calls=%async_computation.3 | async-start | bytes 2064384 | tf_op jit(solution)/shard_map/all_gather | solution.py:83
  74.4 196.5 %all-gather.5.cloned.1.call-start = ((), (), s32[]{:S(2)}) async-start(), calls=%async_computation.2 | async-start | bytes 2064384 | tf_op jit(solution)/shard_map/all_gather | solution.py:126
  228.8 4.8 %copy-start.1 = (bf16[2,64,896]{2,1,0:T(8,128)(2,1)S(1)}, bf16[2,64,896]{2,1,0:T(8,128)(2,1)}, u32[]{:S(2)}) copy-start(bf16[2,64,896]{2,1,0:T(8,128)(2,1)} %param.11) | copy-start | bytes 688132
  270.9 3.1 %copy-start = (bf16[512,1792]{1,0:T(8,128)(2,1)S(1)}, bf16[512,1792]{1,0:T(8,128)(2,1)}, u32[]{:S(2)}) copy-start(bf16[512,1792]{1,0:T(8,128)(2,1)} %all-gather.5.cloned.1.call-done) | copy-start | bytes 5505028
Sparse Core Ops, SparseCore 0:
  74.5 86.5 all-gather.6
  228.1 42.7 all-gather.4
